TPU v7x, 32 devices: a whole 2x2x4 slice. The times are simulated.
32 devices in a mesh: dp: 8 (over y, x, core), ffn: 4 (over z).
Axes of the slice: x: 2, y: 2, z: 4, core: 2. Of those that a mesh axis runs over, the one named last changes fastest.
Arguments:
- layer_activations: bfloat16 [64, 512, 768], P(('dp', 'ffn')), may hold values from -6 to 6
- token_counts_each: int32 [64], P(('dp', 'ffn')), may hold values from 64 to 512, as said below
- attention_triple_matrix: bfloat16 [768, 2304], P('dp', 'ffn'), may hold values from -0.21875 to 0.21875
- attention_final_matrix: bfloat16 [768, 768], P('dp', 'ffn'), may hold values from -1.75 to 1.75
- feedfwd_expand_matrix: bfloat16 [768, 3072], P('dp', 'ffn'), may hold values from -0.21875 to 0.21875
- feedfwd_expand_offset: bfloat16 [3072], P('ffn'), may hold values from -3 to 3
- feedfwd_contract_matrix: bfloat16 [3072, 768], P('ffn', 'dp'), may hold values from -0.109375 to 0.109375
- layernorm_scales: bfloat16 [2, 768], P(None, 'dp'), may hold values from 0.25 to 1.75
- offset_vectors: bfloat16 [6, 768], P(None, 'dp'), may hold values from -2 to 2
- learned_gate_scores: bfloat16 [512, 512], P('dp', 'ffn'), may hold values from -5 to 5
- fixed_jitter_matrix: bfloat16 [512, 512], P('dp', 'ffn'), may hold values from -1 to 1
- relaxation_heat: float32 [1], replicated, may hold values from 0.67 to 1
- loss_grad_result: bfloat16 [64, 512, 768], P(('dp', 'ffn')), may hold values from -6 to 6
Outputs:
- outputs: bfloat16 [64, 512, 768], P(('dp', 'ffn'))
- grad_inputs: float32 [64, 512, 768], P(('dp', 'ffn'))
- grad_w_qkv: float32 [768, 2304], P('dp', 'ffn')
- grad_w_out: float32 [768, 768], P('dp', 'ffn')
- grad_w_up: float32 [768, 3072], P('dp', 'ffn')
- grad_b_up: float32 [3072], P('ffn')
- grad_w_down: float32 [3072, 768], P('ffn', 'dp')
- grad_gains: float32 [2, 768], P(None, 'dp')
- grad_shifts: float32 [6, 768], P(None, 'dp')
- grad_logits: float32 [512, 512], P('dp', 'ffn')
Inputs may be any that keep to these rules, and one draw needn't show every extreme that they name: `token_counts_each`: number of real tokens of a sequence; the other positions of its 512 are padding, and only key positions are masked; some sequence has exactly 512 and some exactly 64.
All inputs are finite; a program needn't handle non-finite values.
Results may differ from a plain program's by a relative error of at most 0.012.
The roundings to bfloat16 on the way count: a program that leaves them out, or rounds other values in their place, can miss the bound.
Values may be sent and summed in bfloat16 or wider, within the bound.
A program may use at most 192 MiB of HBM per device.

v0:
```python
import jax
import jax.numpy as jnp
from jax import lax
from jax.sharding import PartitionSpec as P

D = 768
HEADS = 12
HEAD_DIM = 64
SEQ_LEN = 512
MICRO = 2
norm_eps = 1e-06


def split_up(value, dim, size):
    dims = value.shape
    parts = value.reshape(*dims[:dim], size, dims[dim] // size, *dims[dim + 1 :])
    return jnp.moveaxis(parts, dim, 0)


def summed_on_arrival(value, axis, dim):
    parts = split_up(value, dim, lax.axis_size(axis))
    arrived = lax.all_to_all(parts, axis, split_axis=0, concat_axis=0, tiled=True)
    return arrived.astype(jnp.float32).sum(axis=0)


def assemble(tile_stack, rows_dp, cols_ffn):
    count_all, first_len, second_len = tile_stack.shape
    grid = tile_stack.reshape(rows_dp, cols_ffn, first_len, second_len)
    return grid.transpose(0, 2, 1, 3).reshape(rows_dp * first_len, cols_ffn * second_len)


def disperse(full_grad, rows_dp, cols_ffn):
    total_rows, total_cols = full_grad.shape
    grid = full_grad.reshape(rows_dp, total_rows // rows_dp, cols_ffn, total_cols // cols_ffn)
    return grid.transpose(0, 2, 1, 3).reshape(
        rows_dp * cols_ffn, total_rows // rows_dp, total_cols // cols_ffn
    )


def vector_join(tile_stack, rows_dp, cols_ffn):
    count_all, kinds_count, part_len = tile_stack.shape
    picked = tile_stack.reshape(rows_dp, cols_ffn, kinds_count, part_len)[:, 0]
    return picked.transpose(1, 0, 2).reshape(kinds_count, rows_dp * part_len)


def vector_split(full_grad, rows_dp, cols_ffn):
    kinds_count, width_all = full_grad.shape
    part_len = width_all // rows_dp
    pieces = full_grad.reshape(kinds_count, rows_dp, part_len).transpose(1, 0, 2)
    spread = jnp.broadcast_to(pieces[:, None], (rows_dp, cols_ffn, kinds_count, part_len))
    return spread.reshape(rows_dp * cols_ffn, kinds_count, part_len)


def dot_first(left, right):
    return lax.dot_general(
        left, right, (((0,), (0,)), ((), ())), preferred_element_type=jnp.float32
    )


def dot_last(left, right):
    return lax.dot_general(
        left, right, (((1,), (1,)), ((), ())), preferred_element_type=jnp.float32
    )


def layer_norm(values, gain, shift):
    mean_row = jnp.mean(values, axis=-1, keepdims=True)
    centered = values - mean_row
    inv_std = lax.rsqrt(jnp.mean(centered * centered, axis=-1, keepdims=True) + norm_eps)
    normed = centered * inv_std
    return (normed * gain + shift, normed, inv_std)


def norm_back(grad_out, normed, inv_std, gain):
    grad_normed = grad_out * gain
    grad_in = inv_std * (
        grad_normed
        - jnp.mean(grad_normed, axis=-1, keepdims=True)
        - normed * jnp.mean(grad_normed * normed, axis=-1, keepdims=True)
    )
    return (grad_in, jnp.sum(grad_out * normed, axis=0), jnp.sum(grad_out, axis=0))


def gelu_slope(values):
    return (
        0.5 * (1.0 + lax.erf(values * 0.7071067811865476))
        + values * jnp.exp(-0.5 * values * values) * 0.3989422804014327
    )


def score_block(queries, keys_low, natural_log_gate, live):
    scores = (
        jnp.einsum("sqhd,skhd->shqk", queries, keys_low, preferred_element_type=jnp.float32)
        * HEAD_DIM ** (-0.5)
        + natural_log_gate
    )
    return jnp.where(live[:, None, None, :], scores, -1e30)


def attend(queries, keys_low, values_low, natural_log_gate, live):
    scores = score_block(queries, keys_low, natural_log_gate, live)
    peak = jnp.max(scores, axis=-1, keepdims=True)
    shifted_exp = jnp.exp(scores - peak)
    total_exp = jnp.sum(shifted_exp, axis=-1, keepdims=True)
    probs_low = (shifted_exp / total_exp).astype(jnp.bfloat16)
    context = jnp.einsum(
        "shqk,skhd->sqhd", probs_low, values_low, preferred_element_type=jnp.float32
    )
    return (context, peak + jnp.log(total_exp))


def attend_back(queries, keys_low, values_low, natural_log_gate, live, log_total, grad_context):
    scores = score_block(queries, keys_low, natural_log_gate, live)
    probs = jnp.exp(scores - log_total)
    grad_probs = jnp.einsum(
        "sqhd,skhd->shqk", grad_context, values_low, preferred_element_type=jnp.float32
    )
    grad_values = jnp.einsum(
        "shqk,sqhd->skhd",
        probs.astype(jnp.bfloat16),
        grad_context,
        preferred_element_type=jnp.float32,
    )
    grad_scores = probs * (grad_probs - jnp.sum(probs * grad_probs, axis=-1, keepdims=True))
    grad_mask = jnp.sum(grad_scores, axis=(0, 1))
    grad_scores_low = grad_scores.astype(jnp.bfloat16)
    grad_queries = jnp.einsum(
        "shqk,skhd->sqhd", grad_scores_low, keys_low, preferred_element_type=jnp.float32
    ) * HEAD_DIM ** (-0.5)
    grad_keys = jnp.einsum(
        "shqk,sqhd->skhd", grad_scores_low, queries, preferred_element_type=jnp.float32
    ) * HEAD_DIM ** (-0.5)
    return (grad_queries, grad_keys, grad_values, grad_mask)


def fetch_weights(
    attention_triple_matrix,
    attention_final_matrix,
    feedfwd_expand_matrix,
    feedfwd_contract_matrix,
    layernorm_scales,
    offset_vectors,
    learned_gate_scores,
    fixed_jitter_matrix,
    relaxation_heat,
):
    rows_dp = lax.axis_size("dp")
    cols_ffn = lax.axis_size("ffn")
    tiles = (
        lax.all_gather(attention_triple_matrix[None], ("dp", "ffn"), axis=0, tiled=True),
        lax.all_gather(attention_final_matrix[None], ("dp", "ffn"), axis=0, tiled=True),
        lax.all_gather(learned_gate_scores[None], ("dp", "ffn"), axis=0, tiled=True),
        lax.all_gather(fixed_jitter_matrix[None], ("dp", "ffn"), axis=0, tiled=True),
        lax.all_gather(layernorm_scales[None], ("dp", "ffn"), axis=0, tiled=True),
        lax.all_gather(offset_vectors[None], ("dp", "ffn"), axis=0, tiled=True),
    )
    ffn_parts = (
        lax.all_gather(feedfwd_expand_matrix, "dp", axis=0, tiled=True),
        lax.all_gather(feedfwd_contract_matrix, "dp", axis=1, tiled=True),
    )
    combined_attention_scores = (
        assemble(tiles[2], rows_dp, cols_ffn).astype(jnp.float32)
        + assemble(tiles[3], rows_dp, cols_ffn).astype(jnp.float32)
    ) / relaxation_heat[0]
    natural_log_gate = jax.nn.log_sigmoid(combined_attention_scores)
    gate_sharpness = jax.nn.sigmoid(-combined_attention_scores) / relaxation_heat[0]
    return (
        assemble(tiles[0], rows_dp, cols_ffn),
        assemble(tiles[1], rows_dp, cols_ffn),
        natural_log_gate,
        gate_sharpness,
        vector_join(tiles[4], rows_dp, cols_ffn).astype(jnp.float32),
        vector_join(tiles[5], rows_dp, cols_ffn).astype(jnp.float32),
        ffn_parts[0],
        ffn_parts[1],
    )


def reduce_grads(local_grads):
    rows_dp = lax.axis_size("dp")
    cols_ffn = lax.axis_size("ffn")
    grad_qkv, grad_out, grad_logit, grad_gain, grad_shift, grad_up, grad_down, grad_bias_up = (
        local_grads
    )
    attn_parts = (
        lax.psum_scatter(
            disperse(grad_qkv, rows_dp, cols_ffn), ("dp", "ffn"), scatter_dimension=0, tiled=True
        ),
        lax.psum_scatter(
            disperse(grad_out, rows_dp, cols_ffn), ("dp", "ffn"), scatter_dimension=0, tiled=True
        ),
        lax.psum_scatter(
            disperse(grad_logit, rows_dp, cols_ffn), ("dp", "ffn"), scatter_dimension=0, tiled=True
        ),
        lax.psum_scatter(
            vector_split(grad_gain, rows_dp, cols_ffn),
            ("dp", "ffn"),
            scatter_dimension=0,
            tiled=True,
        ),
        lax.psum_scatter(
            vector_split(grad_shift, rows_dp, cols_ffn),
            ("dp", "ffn"),
            scatter_dimension=0,
            tiled=True,
        ),
    )
    bias_rows = jnp.broadcast_to(grad_bias_up[None], (rows_dp, grad_bias_up.shape[0]))
    ffn_parts = (
        summed_on_arrival(grad_up.astype(jnp.bfloat16), "dp", 0),
        summed_on_arrival(grad_down.astype(jnp.bfloat16), "dp", 1),
        summed_on_arrival(bias_rows.astype(jnp.bfloat16), "dp", 0),
    )
    return (
        attn_parts[0][0],
        attn_parts[1][0],
        attn_parts[2][0],
        attn_parts[3][0],
        attn_parts[4][0],
        ffn_parts[0],
        ffn_parts[1],
        ffn_parts[2][0],
    )


def micro_step(fetched, inputs_block, lengths_block, cot_block, feedfwd_expand_offset):
    (
        full_qkv,
        full_out,
        natural_log_gate,
        gate_sharpness,
        gains_full,
        shifts_full,
        full_up,
        full_down,
    ) = fetched
    seq_count = inputs_block.shape[0]
    row_count = seq_count * SEQ_LEN
    flat_in = inputs_block.reshape(row_count, D)
    qkv_bias = jnp.concatenate([shifts_full[0], jnp.zeros((D,), jnp.float32), shifts_full[1]])
    proj_low = (jnp.dot(flat_in, full_qkv, preferred_element_type=jnp.float32) + qkv_bias).astype(
        jnp.bfloat16
    )
    head_shape = (seq_count, SEQ_LEN, HEADS, HEAD_DIM)
    queries = proj_low[:, :D].reshape(head_shape)
    keys_low = proj_low[:, D : 2 * D].reshape(head_shape)
    values_low = proj_low[:, 2 * D :].reshape(head_shape)
    live = lax.broadcasted_iota(jnp.int32, (seq_count, SEQ_LEN), 1) < lengths_block[:, None]
    context, log_total = attend(queries, keys_low, values_low, natural_log_gate, live)
    context_low = context.reshape(row_count, D).astype(jnp.bfloat16)
    first_sum = (
        flat_in.astype(jnp.float32)
        + jnp.dot(context_low, full_out, preferred_element_type=jnp.float32)
        + shifts_full[2]
    )
    hidden, normed_one, inv_one = layer_norm(first_sum, gains_full[0], shifts_full[4])
    hidden_low = hidden.astype(jnp.bfloat16)
    gathered = lax.all_gather(hidden_low, "ffn", axis=0, tiled=True)
    pre_act = jnp.dot(
        gathered, full_up, preferred_element_type=jnp.float32
    ) + feedfwd_expand_offset.astype(jnp.float32)
    act_low = jax.nn.gelu(pre_act, approximate=False).astype(jnp.bfloat16)
    partial_out = jnp.dot(act_low, full_down, preferred_element_type=jnp.float32)
    ffn_out = lax.psum_scatter(partial_out, "ffn", scatter_dimension=0, tiled=True)
    second_sum = hidden + ffn_out + shifts_full[3]
    result, normed_two, inv_two = layer_norm(second_sum, gains_full[1], shifts_full[5])
    cot_flat = cot_block.reshape(row_count, D).astype(jnp.float32)
    grad_second, grad_gain_two, grad_shift_two = norm_back(
        cot_flat, normed_two, inv_two, gains_full[1]
    )
    grad_second_low = grad_second.astype(jnp.bfloat16)
    grad_gathered = lax.all_gather(grad_second_low, "ffn", axis=0, tiled=True)
    grad_w_down = dot_first(act_low, grad_gathered)
    grad_act = dot_last(grad_gathered, full_down)
    grad_pre = (grad_act * gelu_slope(pre_act)).astype(jnp.bfloat16)
    grad_bias_up = jnp.sum(grad_pre, axis=0, dtype=jnp.float32)
    grad_w_up = dot_first(gathered, grad_pre)
    grad_hidden_part = dot_last(grad_pre, full_up)
    grad_hidden_ffn = lax.psum_scatter(grad_hidden_part, "ffn", scatter_dimension=0, tiled=True)
    grad_hidden = grad_second + grad_hidden_ffn
    grad_first, grad_gain_one, grad_shift_one = norm_back(
        grad_hidden, normed_one, inv_one, gains_full[0]
    )
    grad_first_low = grad_first.astype(jnp.bfloat16)
    grad_w_out = dot_first(context_low, grad_first_low)
    grad_context = dot_last(grad_first_low, full_out).astype(jnp.bfloat16).reshape(head_shape)
    grad_queries, grad_keys, grad_values, grad_mask = attend_back(
        queries, keys_low, values_low, natural_log_gate, live, log_total, grad_context
    )
    grad_projected = jnp.concatenate(
        [
            grad_queries.reshape(row_count, D).astype(jnp.bfloat16),
            grad_keys.reshape(row_count, D).astype(jnp.bfloat16),
            grad_values.reshape(row_count, D).astype(jnp.bfloat16),
        ],
        axis=1,
    )
    grad_w_qkv = dot_first(flat_in, grad_projected)
    grad_inputs = grad_first + dot_last(grad_projected, full_qkv)
    grad_query_bias = jnp.sum(grad_projected[:, :D], axis=0, dtype=jnp.float32)
    grad_value_bias = jnp.sum(grad_projected[:, 2 * D :], axis=0, dtype=jnp.float32)
    grad_shift_all = jnp.stack(
        [
            grad_query_bias,
            grad_value_bias,
            jnp.sum(grad_first, axis=0),
            jnp.sum(grad_second, axis=0),
            grad_shift_one,
            grad_shift_two,
        ]
    )
    grad_gain_all = jnp.stack([grad_gain_one, grad_gain_two])
    grad_logit = grad_mask * gate_sharpness
    local_grads = (
        grad_w_qkv,
        grad_w_out,
        grad_logit,
        grad_gain_all,
        grad_shift_all,
        grad_w_up,
        grad_w_down,
        grad_bias_up,
    )
    return (
        result.astype(jnp.bfloat16).reshape(seq_count, SEQ_LEN, D),
        grad_inputs.reshape(seq_count, SEQ_LEN, D),
        local_grads,
    )


def on_device(
    layer_activations,
    token_counts_each,
    attention_triple_matrix,
    attention_final_matrix,
    feedfwd_expand_matrix,
    feedfwd_expand_offset,
    feedfwd_contract_matrix,
    layernorm_scales,
    offset_vectors,
    learned_gate_scores,
    fixed_jitter_matrix,
    relaxation_heat,
    loss_grad_result,
):
    seq_block = layer_activations.shape[0] // MICRO
    result_list = []
    grad_list = []
    summed = None
    for micro_index in range(MICRO):
        fetched = fetch_weights(
            attention_triple_matrix,
            attention_final_matrix,
            feedfwd_expand_matrix,
            feedfwd_contract_matrix,
            layernorm_scales,
            offset_vectors,
            learned_gate_scores,
            fixed_jitter_matrix,
            relaxation_heat,
        )
        begin = micro_index * seq_block
        result_block, grad_block, local_grads = micro_step(
            fetched,
            layer_activations[begin : begin + seq_block],
            token_counts_each[begin : begin + seq_block],
            loss_grad_result[begin : begin + seq_block],
            feedfwd_expand_offset,
        )
        result_list.append(result_block)
        grad_list.append(grad_block)
        reduced = reduce_grads(local_grads)
        if summed is None:
            summed = reduced
        else:
            summed = tuple((left + right for left, right in zip(summed, reduced)))
    return (
        jnp.concatenate(result_list, axis=0),
        jnp.concatenate(grad_list, axis=0),
        summed[0],
        summed[1],
        summed[5],
        summed[7],
        summed[6],
        summed[3],
        summed[4],
        summed[2],
    )


def solution(mesh):
    in_specs = (
        P(("dp", "ffn"), None, None),
        P(("dp", "ffn")),
        P("dp", "ffn"),
        P("dp", "ffn"),
        P("dp", "ffn"),
        P("ffn"),
        P("ffn", "dp"),
        P(None, "dp"),
        P(None, "dp"),
        P("dp", "ffn"),
        P("dp", "ffn"),
        P(),
        P(("dp", "ffn"), None, None),
    )
    out_specs = (
        P(("dp", "ffn"), None, None),
        P(("dp", "ffn"), None, None),
        P("dp", "ffn"),
        P("dp", "ffn"),
        P("dp", "ffn"),
        P("ffn"),
        P("ffn", "dp"),
        P(None, "dp"),
        P(None, "dp"),
        P("dp", "ffn"),
    )
    return jax.shard_map(
        on_device, mesh=mesh, in_specs=in_specs, out_specs=out_specs, check_vma=False
    )
```

profile of v0, /device:TPU:0, one launch (start us, length us, event | category | flops | bytes accessed | tf_op | source)
XLA Modules:
  0.0 1699.8 jit_solution(4556506373768897747)
XLA Ops:
  13.2 69.5 %all-gather.7 = bf16[32,2,96]{2,1,0:T(2,128)(2,1)S(1)} all-gather(bf16[1,2,96]{2,1,0:T(2,128)(2,1)} %bitcast.336), channel_id=7, replica_groups=mesh['dp'=8,'ffn'=4] {'dp','ffn'}, dimensions={0}, use_global_device_ids=true | all-gather | bytes 12672 | tf_op jit(solution)/shard_map/all_gather | solution.py:154
  82.7 64.6 %all-gather.6 = bf16[32,6,96]{2,1,0:T(8,128)(2,1)S(1)} all-gather(bf16[1,6,96]{2,1,0:T(8,128)(2,1)} %bitcast.335), channel_id=3, replica_groups=mesh['dp'=8,'ffn'=4] {'dp','ffn'}, dimensions={0}, use_global_device_ids=true | all-gather | bytes 38016 | tf_op jit(solution)/shard_map/all_gather | solution.py:155
  148.4 70.6 %all-gather.2 = bf16[2048,128]{1,0:T(8,128)(2,1)S(1)} all-gather(bf16[64,128]{1,0:T(8,128)(2,1)} %param.22), channel_id=4, replica_groups=mesh['dp'=8,'ffn'=4] {'dp','ffn'}, dimensions={0}, use_global_device_ids=true | all-gather | bytes 540672 | tf_op jit(solution)/shard_map/all_gather | solution.py:152
  219.0 68.3 %all-gather.3 = bf16[2048,128]{1,0:T(8,128)(2,1)S(1)} all-gather(bf16[64,128]{1,0:T(8,128)(2,1)} %param.23), channel_id=5, replica_groups=mesh['dp'=8,'ffn'=4] {'dp','ffn'}, dimensions={0}, use_global_device_ids=true | all-gather | bytes 540672 | tf_op jit(solution)/shard_map/all_gather | solution.py:153
  355.1 59.9 %all-gather.23.cloned.1.call-done = bf16[2048,768]{1,0:T(8,128)(2,1)} async-done(((bf16[512,768]{1,0:T(8,128)(2,1)}), bf16[2048,768]{1,0:T(8,128)(2,1)}) %all-gather.23.cloned.1.call-update) | async-done | bytes 3145744 | tf_op jit(solution)/shard_map/all_gather | solution.py:258
  422.5 56.6 %all-gather.17.cloned.1.call-done = bf16[2048,768]{1,0:T(8,128)(2,1)} async-done(((bf16[512,768]{1,0:T(8,128)(2,1)}), bf16[2048,768]{1,0:T(8,128)(2,1)}) %all-gather.17.cloned.1.call-update) | async-done | bytes 3145744 | tf_op jit(solution)/shard_map/all_gather | solution.py:258
  479.2 32.5 %fusion.6 = (bf16[2048,768]{1,0:T(8,128)(2,1)}, bf16[2048,768]{1,0:T(8,128)(2,1)}, f32[2048,768]{1,0:T(8,128)}) fusion(f32[768]{0:T(1024)S(1)} %convert_element_type.336, f32[2048,768]{1,0:T(8,128)} %fusion.120, bf16[2048,768]{1,0:T(8,128)(2,1)} %all-gather.17.cloned.1.call-done, bf16[768,768]{1,0:T(8,128)(2,1)} %all-gather.19.cloned.1.call-done), kind=kOutput, calls=%fused_computation.23 | convolution fusion | flops 2623537152 | bytes 23202816 | tf_op jit(solution)/shard_map/dot_general | solution.py:259
  527.7 101.1 %reduce-scatter.8.cloned.1.call-done = f32[512,768]{1,0:T(8,128)} async-done(((f32[2048,768]{1,0:T(8,128)}), f32[512,768]{1,0:T(8,128)}) %reduce-scatter.8.cloned.1.call-update) | async-done | bytes 1572880 | tf_op jit(solution)/shard_map/reduce_scatter | solution.py:264
  628.8 113.6 %reduce-scatter.10.cloned.1.call-done = f32[512,768]{1,0:T(8,128)} async-done(((f32[2048,768]{1,0:T(8,128)}), f32[512,768]{1,0:T(8,128)}) %reduce-scatter.10.cloned.1.call-update) | async-done | bytes 1572880 | tf_op jit(solution)/shard_map/reduce_scatter | solution.py:264
  756.4 61.5 %all-gather.25.cloned.1.call-done = bf16[2048,768]{1,0:T(8,128)(2,1)} async-done(((bf16[512,768]{1,0:T(8,128)(2,1)}), bf16[2048,768]{1,0:T(8,128)(2,1)}) %all-gather.25.cloned.1.call-update) | async-done | bytes 3145744 | tf_op jit(solution)/shard_map/all_gather | solution.py:272
  831.6 49.8 %all-gather.27.cloned.1.call-done = bf16[2048,768]{1,0:T(8,128)(2,1)} async-done(((bf16[512,768]{1,0:T(8,128)(2,1)}), bf16[2048,768]{1,0:T(8,128)(2,1)}) %all-gather.27.cloned.1.call-update) | async-done | bytes 3145744 | tf_op jit(solution)/shard_map/all_gather | solution.py:272
  897.4 95.8 %reduce-scatter.12.cloned.1.call-done = f32[512,768]{1,0:T(8,128)} async-done(((f32[2048,768]{1,0:T(8,128)}), f32[512,768]{1,0:T(8,128)}) %reduce-scatter.12.cloned.1.call-update) | async-done | bytes 1572880 | tf_op jit(solution)/shard_map/reduce_scatter | solution.py:279
  997.0 109.7 %reduce-scatter.14.cloned.1.call-done = f32[512,768]{1,0:T(8,128)} async-done(((f32[2048,768]{1,0:T(8,128)}), f32[512,768]{1,0:T(8,128)}) %reduce-scatter.14.cloned.1.call-update) | async-done | bytes 1572880 | tf_op jit(solution)/shard_map/reduce_scatter | solution.py:279
  1120.7 8.9 multiply_reduce_fusion.1
  1148.9 13.7 fusion.46
  1172.6 13.6 fusion.48
  1234.5 10.4 reshape.651
  1283.5 10.3 all-to-all-done.5
  1304.7 10.5 all-to-all-done.1
  1326.1 10.4 all-to-all-done.4
  1360.5 39.7 %all-reduce = f32[32,2,96]{2,1,0:T(2,128)S(1)} all-reduce(f32[32,2,96]{2,1,0:T(2,128)S(1)} %bitcast.332), channel_id=19, replica_groups=mesh['dp'=8,'ffn'=4] {'dp','ffn'}, use_global_device_ids=true, to_apply=%region_40.41.clone | all-reduce | flops 6144 | bytes 49152
  1411.2 48.5 %reduce-scatter.20.cloned.1.call-done = f32[1,64,128]{2,1,0:T(8,128)} async-done(((f32[32,64,128]{2,1,0:T(8,128)}), f32[1,64,128]{2,1,0:T(8,128)}) %reduce-scatter.20.cloned.1.call-update) | async-done | bytes 32784 | tf_op jit(solution)/shard_map/reduce_scatter | solution.py:192
  1459.7 104.6 %reduce-scatter.18.cloned.1.call-done = f32[1,96,192]{2,1,0:T(8,128)} async-done(((f32[32,96,192]{2,1,0:T(8,128)}), f32[1,96,192]{2,1,0:T(8,128)}) %reduce-scatter.18.cloned.1.call-update) | async-done | bytes 73744 | tf_op jit(solution)/shard_map/reduce_scatter | solution.py:189
  1564.2 128.5 %reduce-scatter.16.cloned.1.call-done = f32[1,96,576]{2,1,0:T(8,128)} async-done(((f32[32,96,576]{2,1,0:T(8,128)}), f32[1,96,576]{2,1,0:T(8,128)}) %reduce-scatter.16.cloned.1.call-update) | async-done | bytes 221200 | tf_op jit(solution)/shard_map/reduce_scatter | solution.py:186
  (328 shorter events, 331.0 us)
Async XLA Ops:
  7.2 284.6 %all-gather.31.cloned.1.call-start = ((), (), s32[]{:S(2)}) async-start(), calls=%async_computation.24 | async-start | bytes 1622016 | tf_op jit(solution)/shard_map/all_gather | solution.py:151
  7.9 288.0 %all-gather.29.cloned.1.call-start = ((), (), s32[]{:S(2)}) async-start(), calls=%async_computation.23 | async-start | bytes 4055040 | tf_op jit(solution)/shard_map/all_gather | solution.py:150
  8.7 346.4 %all-gather.19.cloned.1.call-start = ((), (), s32[]{:S(2)}) async-start(), calls=%async_computation.14 | async-start | bytes 1327104 | tf_op jit(solution)/shard_map/all_gather | solution.py:158
  9.4 405.6 %all-gather.23.cloned.1.call-start = ((), (), s32[]{:S(2)}) async-start(), calls=%async_computation.17 | async-start | bytes 3932160 | tf_op jit(solution)/shard_map/all_gather | solution.py:258
  317.9 26.2 %copy-start.12 = (bf16[512,768]{0,1:T(8,128)(2,1)}, bf16[512,768]{0,1:T(8,128)(2,1)S(1)}, u32[]{:S(2)}) copy-start(bf16[512,768]{0,1:T(8,128)(2,1)S(1)} %copy.194) | copy-start | bytes 2359300
  353.8 125.4 %all-gather.17.cloned.1.call-start = ((), (), s32[]{:S(2)}) async-start(), calls=%async_computation.13 | async-start | bytes 3932160 | tf_op jit(solution)/shard_map/all_gather | solution.py:258
  354.4 157.3 %all-gather.21.cloned.1.call-start = ((), (), s32[]{:S(2)}) async-start(), calls=%async_computation.15 | async-start | bytes 1327104 | tf_op jit(solution)/shard_map/all_gather | solution.py:159
  355.0 273.8 %reduce-scatter.8.cloned.1.call-start = ((), (), s32[]{:S(2)}) async-start(), calls=%async_computation.16 | async-start | bytes 7864320 | tf_op jit(solution)/shard_map/reduce_scatter | solution.py:264
  519.2 223.2 %reduce-scatter.10.cloned.1.call-start = ((), (), s32[]{:S(2)}) async-start(), calls=%async_computation.18 | async-start | bytes 7864320 | tf_op jit(solution)/shard_map/reduce_scatter | solution.py:264
  526.8 291.1 %all-gather.25.cloned.1.call-start = ((), (), s32[]{:S(2)}) async-start(), calls=%async_computation.19 | async-start | bytes 3932160 | tf_op jit(solution)/shard_map/all_gather | solution.py:272
  753.7 127.8 %all-gather.27.cloned.1.call-start = ((), (), s32[]{:S(2)}) async-start(), calls=%async_computation.21 | async-start | bytes 3932160 | tf_op jit(solution)/shard_map/all_gather | solution.py:272
  756.3 236.9 %reduce-scatter.12.cloned.1.call-start = ((), (), s32[]{:S(2)}) async-start(), calls=%async_computation.20 | async-start | bytes 7864320 | tf_op jit(solution)/shard_map/reduce_scatter | solution.py:279
  831.6 275.1 %reduce-scatter.14.cloned.1.call-start = ((), (), s32[]{:S(2)}) async-start(), calls=%async_computation.22 | async-start | bytes 7864320 | tf_op jit(solution)/shard_map/reduce_scatter | solution.py:279
  895.3 514.6 %all-reduce.4.cloned.1.call-start = ((), (), s32[]{:S(2)}) async-start(), calls=%async_computation.28 | async-start | bytes 262144
  1196.2 263.5 %reduce-scatter.20.cloned.1.call-start = ((), (), s32[]{:S(2)}) async-start(), calls=%async_computation.27 | async-start | bytes 1081344 | tf_op jit(solution)/shard_map/reduce_scatter | solution.py:192
  1200.2 364.0 %reduce-scatter.18.cloned.1.call-start = ((), (), s32[]{:S(2)}) async-start(), calls=%async_computation.26 | async-start | bytes 3244032 | tf_op jit(solution)/shard_map/reduce_scatter | solution.py:189
  1210.3 482.4 %reduce-scatter.16.cloned.1.call-start = ((), (), s32[]{:S(2)}) async-start(), calls=%async_computation.25 | async-start | bytes 8110080 | tf_op jit(solution)/shard_map/reduce_scatter | solution.py:186
  1254.1 8.4 all-to-all-start.3
  1262.4 10.0 all-to-all-start.2
  1272.4 21.4 %all-to-all-start.5 = ((bf16[8,768,96]{1,2,0:T(8,128)(2,1)}), bf16[8,768,96]{1,2,0:T(8,128)(2,1)}, u32[]{:S(2)}, u32[]{:S(2)}) async-start(bf16[8,768,96]{1,2,0:T(8,128)(2,1)} %bitcast.320), calls=%async_computation.9 | async-start | bytes 2359296 | tf_op jit(solution)/shard_map/all_to_all | solution.py:22
  1293.8 21.3 %all-to-all-start.1 = ((bf16[8,96,768]{2,1,0:T(8,128)(2,1)}), bf16[8,96,768]{2,1,0:T(8,128)(2,1)}, u32[]{:S(2)}, u32[]{:S(2)}) async-start(bf16[8,96,768]{2,1,0:T(8,128)(2,1)} %bitcast.321), calls=%async_computation.5 | async-start | bytes 2359296 | tf_op jit(solution)/shard_map/all_to_all | solution.py:22
  1315.2 21.3 %all-to-all-start.4 = ((bf16[8,768,96]{1,2,0:T(8,128)(2,1)}), bf16[8,768,96]{1,2,0:T(8,128)(2,1)}, u32[]{:S(2)}, u32[]{:S(2)}) async-start(bf16[8,768,96]{1,2,0:T(8,128)(2,1)} %bitcast.322), calls=%async_computation.8 | async-start | bytes 2359296 | tf_op jit(solution)/shard_map/all_to_all | solution.py:22
  1336.4 21.6 %all-to-all-start = ((bf16[8,96,768]{2,1,0:T(8,128)(2,1)}), bf16[8,96,768]{2,1,0:T(8,128)(2,1)}, u32[]{:S(2)}, u32[]{:S(2)}) async-start(bf16[8,96,768]{2,1,0:T(8,128)(2,1)} %bitcast.319), calls=%async_computation.4 | async-start | bytes 2359296 | tf_op jit(solution)/shard_map/all_to_all | solution.py:22
  1345.4 55.3 %copy-start.26 = (bf16[12,64,512]{2,1,0:T(8,128)(2,1)S(1)}, bf16[12,64,512]{2,1,0:T(8,128)(2,1)}, u32[]{:S(2)}) copy-start(bf16[12,64,512]{2,1,0:T(8,128)(2,1)} %get-tuple-element.98) | copy-start | bytes 2359300
  (59 other events, 295.1 us)
Sparse Core Ops, SparseCore 0:
  10.9 57.7 all-gather.30
  71.5 60.2 all-gather.28
  133.7 22.7 all-gather.18
  353.9 61.0 all-gather.22
  417.0 62.1 all-gather.16
  480.9 22.7 all-gather.20
  519.4 109.3 reduce-scatter.7
  631.1 111.2 reduce-scatter.9
  753.8 64.0 all-gather.24
  819.3 62.1 all-gather.26
  883.8 109.3 reduce-scatter.11
  995.4 111.2 reduce-scatter.13
  1196.3 124.6 all-reduce.3
  1323.7 135.9 reduce-scatter.19
  1466.4 97.8 reduce-scatter.17
  1571.3 121.4 reduce-scatter.15
where the time goes:
time: 1710 us; the launch traced here: 1700 us
  waiting for transfers between devices  976 us (57%)
  blocking collectives  313 us (18%)
  matrix products  199 us (12%)
  local copies, waits for them, and re-layouts  92 us (5%)
  other arithmetic  78.4 us (5%)
  starting transfers between devices  25.4 us (1%)
    reduce_scatter x2, waiting for transfers between devices, micro_step(): lax.psum_scatter(partial_out, 'ffn', scatter_dimension=0, tiled=True)  215 us
    reduce_scatter x2, waiting for transfers between devices, micro_step(): lax.psum_scatter(grad_hidden_part, 'ffn', scatter_dimension=0, tiled=True)  206 us
    reduce_scatter x1, waiting for transfers between devices, reduce_grads(): lax.psum_scatter(disperse(grad_qkv, rows_dp, cols_ffn), ('dp', 'ffn'), sc...  129 us
    all_gather x2, waiting for transfers between devices, micro_step(): gathered = lax.all_gather(hidden_low, 'ffn', axis=0, tiled=True)  117 us
    all_gather x2, waiting for transfers between devices, micro_step(): grad_gathered = lax.all_gather(grad_second_low, 'ffn', axis=0, tiled=True)  111 us
    reduce_scatter x1, waiting for transfers between devices, reduce_grads(): lax.psum_scatter(disperse(grad_out, rows_dp, cols_ffn), ('dp', 'ffn'), sc...  105 us
    all_gather x1, blocking collectives, fetch_weights(): lax.all_gather(learned_gate_scores[None], ('dp', 'ffn'), axis=0, tiled=True)  70.6 us
    all_gather x1, blocking collectives, fetch_weights(): lax.all_gather(layernorm_scales[None], ('dp', 'ffn'), axis=0, tiled=True)  69.5 us
  transfers between devices with their start and end apart: 22, of which 16 were waited for; matrix products, arithmetic and copies ran while one was open for 15% of the time, Pallas kernels for 0%

commit v1 on v0

--- a/solution.py
+++ b/solution.py
@@ -9,6 +9,18 @@
 SEQ_LEN = 512
 MICRO = 2
 norm_eps = 1e-06
+
+
+def collect(x, axis, dim):
+    ways, here = (lax.axis_size(axis), lax.axis_index(axis))
+    grown, reach = (x, 1)
+    while reach < ways:
+        theirs = lax.ppermute(grown, axis, [(d, d ^ reach) for d in range(ways)])
+        mine_first = jnp.concatenate([grown, theirs], axis=dim)
+        theirs_first = jnp.concatenate([theirs, grown], axis=dim)
+        grown = jnp.where(here & reach == 0, mine_first, theirs_first)
+        reach = 2 * reach
+    return grown
 
 
 def split_up(value, dim, size):
@@ -150,7 +162,7 @@
         lax.all_gather(attention_triple_matrix[None], ("dp", "ffn"), axis=0, tiled=True),
         lax.all_gather(attention_final_matrix[None], ("dp", "ffn"), axis=0, tiled=True),
         lax.all_gather(learned_gate_scores[None], ("dp", "ffn"), axis=0, tiled=True),
-        lax.all_gather(fixed_jitter_matrix[None], ("dp", "ffn"), axis=0, tiled=True),
+        collect(fixed_jitter_matrix[None], ("dp", "ffn"), 0),
         lax.all_gather(layernorm_scales[None], ("dp", "ffn"), axis=0, tiled=True),
         lax.all_gather(offset_vectors[None], ("dp", "ffn"), axis=0, tiled=True),
     )

time: 1710 us -> 1650 us (0.965)
  blocking collectives: 313 us -> 241 us
    all_gather x1 -> x0, blocking collectives: 68.3 us -> none  [fetch_weights(): lax.all_gather(fixed_jitter_matrix[None], ('dp', 'ffn'), axis=0, tiled=True)]
  transfers between devices with their start and end apart: 22 -> 27, of which waited for: 16 -> 18; matrix products, arithmetic and copies ran while one was open for 15% -> 15% of each run, Pallas kernels for 0% -> 0%
where the time goes in v1:
time: 1650 us; the launch traced here: 1640 us
  waiting for transfers between devices  984 us (60%)
  blocking collectives  241 us (15%)
  matrix products  199 us (12%)
  local copies, waits for them, and re-layouts  92 us (6%)
  other arithmetic  79.4 us (5%)
  starting transfers between devices  30.1 us (2%)
    reduce_scatter x2, waiting for transfers between devices, micro_step(): lax.psum_scatter(partial_out, 'ffn', scatter_dimension=0, tiled=True)  215 us
    reduce_scatter x2, waiting for transfers between devices, micro_step(): lax.psum_scatter(grad_hidden_part, 'ffn', scatter_dimension=0, tiled=True)  206 us
    reduce_scatter x1, waiting for transfers between devices, reduce_grads(): lax.psum_scatter(disperse(grad_qkv, rows_dp, cols_ffn), ('dp', 'ffn'), sc...  128 us
    all_gather x2, waiting for transfers between devices, micro_step(): gathered = lax.all_gather(hidden_low, 'ffn', axis=0, tiled=True)  115 us
    all_gather x2, waiting for transfers between devices, micro_step(): grad_gathered = lax.all_gather(grad_second_low, 'ffn', axis=0, tiled=True)  111 us
    reduce_scatter x1, waiting for transfers between devices, reduce_grads(): lax.psum_scatter(disperse(grad_out, rows_dp, cols_ffn), ('dp', 'ffn'), sc...  105 us
    all_gather x1, blocking collectives, fetch_weights(): lax.all_gather(learned_gate_scores[None], ('dp', 'ffn'), axis=0, tiled=True)  69.9 us
    all_gather x1, blocking collectives, fetch_weights(): lax.all_gather(layernorm_scales[None], ('dp', 'ffn'), axis=0, tiled=True)  67.1 us
  transfers between devices with their start and end apart: 27, of which 18 were waited for; matrix products, arithmetic and copies ran while one was open for 15% of the time, Pallas kernels for 0%

profile of v1, /device:TPU:0, one launch (start us, length us, event | category | flops | bytes accessed | tf_op | source)
XLA Modules:
  0.0 1641.7 jit_solution(17114833822983341680)
XLA Ops:
  11.9 67.1 %all-gather.6 = bf16[32,2,96]{2,1,0:T(2,128)(2,1)S(1)} all-gather(bf16[1,2,96]{2,1,0:T(2,128)(2,1)} %bitcast.342), channel_id=6, replica_groups=mesh['dp'=8,'ffn'=4] {'dp','ffn'}, dimensions={0}, use_global_device_ids=true | all-gather | bytes 12672 | tf_op jit(solution)/shard_map/all_gather | solution.py:166
  78.9 64.7 %all-gather.5 = bf16[32,6,96]{2,1,0:T(8,128)(2,1)S(1)} all-gather(bf16[1,6,96]{2,1,0:T(8,128)(2,1)} %bitcast.341), channel_id=3, replica_groups=mesh['dp'=8,'ffn'=4] {'dp','ffn'}, dimensions={0}, use_global_device_ids=true | all-gather | bytes 38016 | tf_op jit(solution)/shard_map/all_gather | solution.py:167
  161.3 69.9 %all-gather.2 = bf16[2048,128]{1,0:T(8,128)(2,1)S(1)} all-gather(bf16[64,128]{1,0:T(8,128)(2,1)} %param.22), channel_id=4, replica_groups=mesh['dp'=8,'ffn'=4] {'dp','ffn'}, dimensions={0}, use_global_device_ids=true | all-gather | bytes 540672 | tf_op jit(solution)/shard_map/all_gather | solution.py:164
  298.4 58.4 %all-gather.22.cloned.1.call-done = bf16[2048,768]{1,0:T(8,128)(2,1)} async-done(((bf16[512,768]{1,0:T(8,128)(2,1)}), bf16[2048,768]{1,0:T(8,128)(2,1)}) %all-gather.22.cloned.1.call-update) | async-done | bytes 3145744 | tf_op jit(solution)/shard_map/all_gather | solution.py:270
  364.4 56.6 %all-gather.16.cloned.1.call-done = bf16[2048,768]{1,0:T(8,128)(2,1)} async-done(((bf16[512,768]{1,0:T(8,128)(2,1)}), bf16[2048,768]{1,0:T(8,128)(2,1)}) %all-gather.16.cloned.1.call-update) | async-done | bytes 3145744 | tf_op jit(solution)/shard_map/all_gather | solution.py:270
  421.1 32.5 %fusion.6 = (bf16[2048,768]{1,0:T(8,128)(2,1)}, bf16[2048,768]{1,0:T(8,128)(2,1)}, f32[2048,768]{1,0:T(8,128)}) fusion(f32[768]{0:T(1024)S(1)} %convert_element_type.336, f32[2048,768]{1,0:T(8,128)} %fusion.121, bf16[2048,768]{1,0:T(8,128)(2,1)} %all-gather.16.cloned.1.call-done, bf16[768,768]{1,0:T(8,128)(2,1)} %all-gather.18.cloned.1.call-done), kind=kOutput, calls=%fused_computation.23 | convolution fusion | flops 2623537152 | bytes 23202816 | tf_op jit(solution)/shard_map/dot_general | solution.py:271
  469.6 101.1 %reduce-scatter.8.cloned.1.call-done = f32[512,768]{1,0:T(8,128)} async-done(((f32[2048,768]{1,0:T(8,128)}), f32[512,768]{1,0:T(8,128)}) %reduce-scatter.8.cloned.1.call-update) | async-done | bytes 1572880 | tf_op jit(solution)/shard_map/reduce_scatter | solution.py:276
  570.7 113.6 %reduce-scatter.10.cloned.1.call-done = f32[512,768]{1,0:T(8,128)} async-done(((f32[2048,768]{1,0:T(8,128)}), f32[512,768]{1,0:T(8,128)}) %reduce-scatter.10.cloned.1.call-update) | async-done | bytes 1572880 | tf_op jit(solution)/shard_map/reduce_scatter | solution.py:276
  698.3 61.5 %all-gather.24.cloned.1.call-done = bf16[2048,768]{1,0:T(8,128)(2,1)} async-done(((bf16[512,768]{1,0:T(8,128)(2,1)}), bf16[2048,768]{1,0:T(8,128)(2,1)}) %all-gather.24.cloned.1.call-update) | async-done | bytes 3145744 | tf_op jit(solution)/shard_map/all_gather | solution.py:284
  773.5 49.8 %all-gather.26.cloned.1.call-done = bf16[2048,768]{1,0:T(8,128)(2,1)} async-done(((bf16[512,768]{1,0:T(8,128)(2,1)}), bf16[2048,768]{1,0:T(8,128)(2,1)}) %all-gather.26.cloned.1.call-update) | async-done | bytes 3145744 | tf_op jit(solution)/shard_map/all_gather | solution.py:284
  839.3 95.8 %reduce-scatter.12.cloned.1.call-done = f32[512,768]{1,0:T(8,128)} async-done(((f32[2048,768]{1,0:T(8,128)}), f32[512,768]{1,0:T(8,128)}) %reduce-scatter.12.cloned.1.call-update) | async-done | bytes 1572880 | tf_op jit(solution)/shard_map/reduce_scatter | solution.py:291
  938.8 109.7 %reduce-scatter.14.cloned.1.call-done = f32[512,768]{1,0:T(8,128)} async-done(((f32[2048,768]{1,0:T(8,128)}), f32[512,768]{1,0:T(8,128)}) %reduce-scatter.14.cloned.1.call-update) | async-done | bytes 1572880 | tf_op jit(solution)/shard_map/reduce_scatter | solution.py:291
  1062.6 8.9 multiply_reduce_fusion.1
  1090.8 13.7 fusion.46
  1114.5 13.6 fusion.48
  1176.4 10.4 reshape.648
  1225.4 10.3 all-to-all-done.5
  1246.6 10.5 all-to-all-done.1
  1267.9 10.4 all-to-all-done.4
  1291.1 8.9 all-to-all-done
  1302.3 39.8 %all-reduce = f32[32,2,96]{2,1,0:T(2,128)S(1)} all-reduce(f32[32,2,96]{2,1,0:T(2,128)S(1)} %bitcast.336), channel_id=18, replica_groups=mesh['dp'=8,'ffn'=4] {'dp','ffn'}, use_global_device_ids=true, to_apply=%region_40.41.clone | all-reduce | flops 6144 | bytes 49152
  1353.1 48.3 %reduce-scatter.20.cloned.1.call-done = f32[1,64,128]{2,1,0:T(8,128)} async-done(((f32[32,64,128]{2,1,0:T(8,128)}), f32[1,64,128]{2,1,0:T(8,128)}) %reduce-scatter.20.cloned.1.call-update) | async-done | bytes 32784 | tf_op jit(solution)/shard_map/reduce_scatter | solution.py:204
  1401.4 104.9 %reduce-scatter.18.cloned.1.call-done = f32[1,96,192]{2,1,0:T(8,128)} async-done(((f32[32,96,192]{2,1,0:T(8,128)}), f32[1,96,192]{2,1,0:T(8,128)}) %reduce-scatter.18.cloned.1.call-update) | async-done | bytes 73744 | tf_op jit(solution)/shard_map/reduce_scatter | solution.py:201
  1506.3 128.4 %reduce-scatter.16.cloned.1.call-done = f32[1,96,576]{2,1,0:T(8,128)} async-done(((f32[32,96,576]{2,1,0:T(8,128)}), f32[1,96,576]{2,1,0:T(8,128)}) %reduce-scatter.16.cloned.1.call-update) | async-done | bytes 221200 | tf_op jit(solution)/shard_map/reduce_scatter | solution.py:198
  (341 shorter events, 336.8 us)
Async XLA Ops:
  7.2 228.0 %all-gather.30.cloned.1.call-start = ((), (), s32[]{:S(2)}) async-start(), calls=%async_computation.24 | async-start | bytes 1622016 | tf_op jit(solution)/shard_map/all_gather | solution.py:163
  7.9 231.4 %all-gather.28.cloned.1.call-start = ((), (), s32[]{:S(2)}) async-start(), calls=%async_computation.23 | async-start | bytes 4055040 | tf_op jit(solution)/shard_map/all_gather | solution.py:162
  8.7 289.8 %all-gather.18.cloned.1.call-start = ((), (), s32[]{:S(2)}) async-start(), calls=%async_computation.14 | async-start | bytes 1327104 | tf_op jit(solution)/shard_map/all_gather | solution.py:170
  8.7 134.9 %collective-permute-start = (bf16[1,64,128]{2,1,0:T(8,128)(2,1)}, bf16[1,64,128]{2,1,0:T(8,128)(2,1)S(1)}, u32[]{:S(2)}, u32[]{:S(2)}) collective-permute-start(bf16[1,64,128]{2,1,0:T(8,128)(2,1)} %bitcast.339), channel_id=1, source_target_pairs={{0,1},{1,0},{2,3},{3,2},{4,5},{5,4},{6,7},{7,6},{8,9},{9,8},{10,11... | collective-permute-start | bytes 49160 | tf_op jit(solution)/shard_map/ppermute | solution.py:18
  11.8 345.1 %all-gather.22.cloned.1.call-start = ((), (), s32[]{:S(2)}) async-start(), calls=%async_computation.17 | async-start | bytes 3932160 | tf_op jit(solution)/shard_map/all_gather | solution.py:270
  157.7 73.5 %collective-permute-start.4 = (bf16[16,64,128]{2,1,0:T(8,128)(2,1)S(1)}, bf16[16,64,128]{2,1,0:T(8,128)(2,1)S(1)}, u32[]{:S(2)}, u32[]{:S(2)}) collective-permute-start(bf16[16,64,128]{2,1,0:T(8,128)(2,1)S(1)} %maximum_select_fusion.1), channel_id=1, source_target_pairs={{0,16},{1,17},{2,18},{3,19},{4,20},{5,21},{6,22},{7,23},{8,24},{9,... | collective-permute-start | bytes 786440 | tf_op jit(solution)/shard_map/ppermute | solution.py:18
  297.2 123.9 %all-gather.16.cloned.1.call-start = ((), (), s32[]{:S(2)}) async-start(), calls=%async_computation.13 | async-start | bytes 3932160 | tf_op jit(solution)/shard_map/all_gather | solution.py:270
  297.8 155.8 %all-gather.20.cloned.1.call-start = ((), (), s32[]{:S(2)}) async-start(), calls=%async_computation.15 | async-start | bytes 1327104 | tf_op jit(solution)/shard_map/all_gather | solution.py:171
  298.3 272.3 %reduce-scatter.8.cloned.1.call-start = ((), (), s32[]{:S(2)}) async-start(), calls=%async_computation.16 | async-start | bytes 7864320 | tf_op jit(solution)/shard_map/reduce_scatter | solution.py:276
  461.1 223.2 %reduce-scatter.10.cloned.1.call-start = ((), (), s32[]{:S(2)}) async-start(), calls=%async_computation.18 | async-start | bytes 7864320 | tf_op jit(solution)/shard_map/reduce_scatter | solution.py:276
  468.7 291.1 %all-gather.24.cloned.1.call-start = ((), (), s32[]{:S(2)}) async-start(), calls=%async_computation.19 | async-start | bytes 3932160 | tf_op jit(solution)/shard_map/all_gather | solution.py:284
  695.6 127.8 %all-gather.26.cloned.1.call-start = ((), (), s32[]{:S(2)}) async-start(), calls=%async_computation.21 | async-start | bytes 3932160 | tf_op jit(solution)/shard_map/all_gather | solution.py:284
  698.2 236.9 %reduce-scatter.12.cloned.1.call-start = ((), (), s32[]{:S(2)}) async-start(), calls=%async_computation.20 | async-start | bytes 7864320 | tf_op jit(solution)/shard_map/reduce_scatter | solution.py:291
  773.5 275.1 %reduce-scatter.14.cloned.1.call-start = ((), (), s32[]{:S(2)}) async-start(), calls=%async_computation.22 | async-start | bytes 7864320 | tf_op jit(solution)/shard_map/reduce_scatter | solution.py:291
  837.2 514.6 %all-reduce.4.cloned.1.call-start = ((), (), s32[]{:S(2)}) async-start(), calls=%async_computation.28 | async-start | bytes 262144
  1138.1 263.3 %reduce-scatter.20.cloned.1.call-start = ((), (), s32[]{:S(2)}) async-start(), calls=%async_computation.27 | async-start | bytes 1081344 | tf_op jit(solution)/shard_map/reduce_scatter | solution.py:204
  1142.1 364.2 %reduce-scatter.18.cloned.1.call-start = ((), (), s32[]{:S(2)}) async-start(), calls=%async_computation.26 | async-start | bytes 3244032 | tf_op jit(solution)/shard_map/reduce_scatter | solution.py:201
  1152.2 482.5 %reduce-scatter.16.cloned.1.call-start = ((), (), s32[]{:S(2)}) async-start(), calls=%async_computation.25 | async-start | bytes 8110080 | tf_op jit(solution)/shard_map/reduce_scatter | solution.py:198
  1196.0 8.4 all-to-all-start.3
  1204.3 10.0 all-to-all-start.2
  1214.3 21.4 %all-to-all-start.5 = ((bf16[8,768,96]{1,2,0:T(8,128)(2,1)}), bf16[8,768,96]{1,2,0:T(8,128)(2,1)}, u32[]{:S(2)}, u32[]{:S(2)}) async-start(bf16[8,768,96]{1,2,0:T(8,128)(2,1)} %bitcast.324), calls=%async_computation.9 | async-start | bytes 2359296 | tf_op jit(solution)/shard_map/all_to_all | solution.py:34
  1235.7 21.3 %all-to-all-start.1 = ((bf16[8,96,768]{2,1,0:T(8,128)(2,1)}), bf16[8,96,768]{2,1,0:T(8,128)(2,1)}, u32[]{:S(2)}, u32[]{:S(2)}) async-start(bf16[8,96,768]{2,1,0:T(8,128)(2,1)} %bitcast.325), calls=%async_computation.5 | async-start | bytes 2359296 | tf_op jit(solution)/shard_map/all_to_all | solution.py:34
  1257.1 21.3 %all-to-all-start.4 = ((bf16[8,768,96]{1,2,0:T(8,128)(2,1)}), bf16[8,768,96]{1,2,0:T(8,128)(2,1)}, u32[]{:S(2)}, u32[]{:S(2)}) async-start(bf16[8,768,96]{1,2,0:T(8,128)(2,1)} %bitcast.326), calls=%async_computation.8 | async-start | bytes 2359296 | tf_op jit(solution)/shard_map/all_to_all | solution.py:34
  1278.3 21.6 %all-to-all-start = ((bf16[8,96,768]{2,1,0:T(8,128)(2,1)}), bf16[8,96,768]{2,1,0:T(8,128)(2,1)}, u32[]{:S(2)}, u32[]{:S(2)}) async-start(bf16[8,96,768]{2,1,0:T(8,128)(2,1)} %bitcast.323), calls=%async_computation.4 | async-start | bytes 2359296 | tf_op jit(solution)/shard_map/all_to_all | solution.py:34
  (64 other events, 389.4 us)
Sparse Core Ops, SparseCore 0:
  10.9 57.7 all-gather.29
  71.5 60.1 all-gather.27
  133.6 23.7 all-gather.17
  297.3 59.5 all-gather.21
  358.9 62.1 all-gather.15
  422.8 22.7 all-gather.19
  461.2 109.3 reduce-scatter.7
  573.0 111.2 reduce-scatter.9
  695.7 64.0 all-gather.23
  761.2 62.1 all-gather.25
  825.7 109.3 reduce-scatter.11
  937.2 111.2 reduce-scatter.13
  1138.2 124.6 all-reduce.3
  1265.6 135.7 reduce-scatter.19
  1408.1 98.1 reduce-scatter.17
  1513.4 121.2 reduce-scatter.15
